TPU v7x, 512 devices: a whole 4x8x8 slice. The times are simulated.
512 devices in a mesh: blk: 64 (over z_hi, y, core), rep: 8 (over z_lo, x).
Axes of the slice: x: 4, y: 8, z: 8 (z_hi: 4, z_lo: 2; z = z_hi * 2 + z_lo), core: 2. Of those that a mesh axis runs over, the one named last changes fastest.
Arguments:
- features: bfloat16 [32768, 128], P('blk'), may hold values from -6 to 6
- weight: bfloat16 [128, 256], replicated, may hold values from -0.5 to 0.5
- tile_vals: bfloat16 [64, 8, 8, 12, 128, 128], P('blk', 'rep'), may hold values from -0.0390625 to 0.0390625
- tile_pos: int32 [64, 8, 8, 12], P('blk', 'rep'), may hold values from 0 to 15, as said below
- tile_count: int32 [64, 8, 8], P('blk', 'rep'), may hold values from 1 to 12, as said below
- cotangent: bfloat16 [32768, 256], P(('blk', 'rep')), may hold values from -6 to 6
Outputs:
- activations: bfloat16 [32768, 256], P(('blk', 'rep'))
- feat_grad: bfloat16 [32768, 128], P(('blk', 'rep'))
- weight_grad: float32 [128, 256], replicated
Inputs may be any that keep to these rules, and one draw needn't show every extreme that they name: `tile_pos`: within one row group, copy and section the entries are distinct. `tile_count`: row group 0 has all 12 slots live in every copy and section.
All inputs are finite; a program needn't handle non-finite values.
Results may differ from a plain program's by a relative error of at most 0.014.
Values may be sent and summed in bfloat16 or wider, within the bound.
A program may use at most 128 MiB of HBM per device.

v0:
```python
import jax
import jax.numpy as jnp
from jax import lax
from jax.sharding import PartitionSpec as P


def gelu_tanh(value):
    return jax.nn.gelu(value, approximate=True)


def skewed(block, sign):
    blks, reps = (lax.axis_size("blk"), lax.axis_size("rep"))
    route = [
        (b * reps + r, (b + sign * r) % blks * reps + r) for b in range(blks) for r in range(reps)
    ]
    return lax.ppermute(block, ("blk", "rep"), route)


def split_dot(left, right):
    high = left.astype(jnp.bfloat16)
    low = (left - high.astype(jnp.float32)).astype(jnp.bfloat16)
    return jnp.dot(high, right, preferred_element_type=jnp.float32) + jnp.dot(
        low, right, preferred_element_type=jnp.float32
    )


def dense_adjacency(tiles, positions, counts, group, blocks):
    sections, slots = positions.shape
    cells = jnp.arange(blocks * blocks, dtype=jnp.int32)
    live = jnp.arange(slots, dtype=jnp.int32)[None, :] < counts[:, None]
    hits = (positions[:, None, :] == cells[None, :, None]) & live[:, None, :]
    slot_of = jnp.argmax(hits, axis=-1).astype(jnp.int32)
    filled = jnp.any(hits, axis=-1)
    order = (group - jnp.arange(sections, dtype=jnp.int32)) % sections
    slot_of, filled = (slot_of[order], filled[order])
    picked = tiles[order[:, None], slot_of]
    return jnp.where(filled[..., None, None], picked, jnp.zeros((), tiles.dtype)).reshape(
        sections, blocks, blocks, tiles.shape[-2], tiles.shape[-1]
    )


def local(features, weight, tile_vals, tile_pos, tile_count, cotangent):
    rep_size = lax.axis_size("rep")
    blk_size = lax.axis_size("blk")
    blk_index = lax.axis_index("blk")
    tile_size = tile_vals.shape[-1]
    rows, feat = features.shape
    blocks = rows // tile_size
    rings = [[r + k * rep_size for k in range(blk_size // rep_size)] for r in range(rep_size)]
    adjacency = dense_adjacency(
        tile_vals[0, 0], tile_pos[0, 0], tile_count[0, 0], blk_index // rep_size, blocks
    )
    gathered = lax.all_gather(skewed(features, 1), "blk", axis_index_groups=rings)
    columns = gathered.reshape(-1, blocks, tile_size, feat)
    mixed = jnp.einsum(
        "jnmik,jmkf->nif", adjacency, columns, preferred_element_type=jnp.float32
    ).reshape(rows, feat)
    mixed = lax.psum_scatter(mixed, "rep", scatter_dimension=0, tiled=True)
    pre = split_dot(mixed, weight)
    outputs, pullback = jax.vjp(gelu_tanh, pre)
    activations = outputs.astype(jnp.bfloat16)
    pre_grad = pullback(cotangent.astype(jnp.float32))[0].astype(jnp.bfloat16)
    weight_grad = lax.dot_general(
        mixed.astype(jnp.bfloat16),
        pre_grad,
        (((0,), (0,)), ((), ())),
        preferred_element_type=jnp.float32,
    )
    weight_grad = lax.psum(lax.psum(weight_grad, "rep"), "blk")
    row_grad = lax.dot_general(
        pre_grad, weight, (((1,), (1,)), ((), ())), preferred_element_type=jnp.float32
    ).astype(jnp.bfloat16)
    row_grad = lax.all_gather(row_grad, "rep", axis=0, tiled=True).reshape(blocks, tile_size, feat)
    partial = jnp.einsum(
        "jnmik,nif->jmkf", adjacency, row_grad, preferred_element_type=jnp.float32
    ).reshape(-1, rows, feat)
    partial = lax.psum_scatter(partial, "blk", scatter_dimension=0, axis_index_groups=rings)
    partial = skewed(partial, -1)
    feat_grad = lax.psum_scatter(partial, "rep", scatter_dimension=0, tiled=True)
    return (activations, feat_grad.astype(jnp.bfloat16), weight_grad)


def solution(mesh):
    placed = (
        P("blk", None),
        P(),
        P("blk", "rep", None, None, None, None),
        P("blk", "rep", None, None),
        P("blk", "rep", None),
        P(("blk", "rep"), None),
    )
    return jax.shard_map(
        local,
        mesh=mesh,
        in_specs=placed,
        out_specs=(P(("blk", "rep"), None), P(("blk", "rep"), None), P()),
        check_vma=False,
    )
```

profile of v0, /device:TPU:1, one launch (start us, length us, event | category | flops | bytes accessed | tf_op | source)
XLA Modules:
  0.0 915.5 jit_solution(509710526468673986)
XLA Ops:
  7.2 1.8 collective-permute-start
  9.0 0.7 copy-done.3
  9.8 0.8 copy.13
  10.6 0.7 iota_compare_fusion.1
  11.2 0.7 iota_reduce_fusion
  11.9 0.6 gather_fusion.1
  12.5 0.1 reshape.130
  12.6 0.1 fusion.13
  12.7 0.6 gather_fusion
  13.3 0.1 copy.14
  13.4 0.1 copy.15
  13.5 3.1 gather_fusion.2
  16.6 3.9 fusion
  20.5 2.3 copy.16
  22.7 72.2 %all-gather.3.cloned.1.call-done = bf16[4096,128]{1,0:T(8,128)(2,1)} async-done(((bf16[512,128]{1,0:T(8,128)(2,1)}), bf16[4096,128]{1,0:T(8,128)(2,1)}) %all-gather.3.cloned.1.call-update) | async-done | bytes 1048592 | tf_op jit(solution)/shard_map/all_gather | solution.py:53
  94.9 4.4 convolution_bitcast_fusion.1
  99.5 6.5 copy.17
  105.9 29.8 %reduce-scatter.4.cloned.1.call-done = f32[64,128]{1,0:T(8,128)} async-done(((f32[512,128]{1,0:T(8,128)}), f32[64,128]{1,0:T(8,128)}) %reduce-scatter.4.cloned.1.call-update) | async-done | bytes 32784 | tf_op jit(solution)/shard_map/reduce_scatter | solution.py:58
  135.7 0.9 fusion.25
  136.6 1.6 fusion.4
  138.3 0.1 convolution_convert_fusion
  138.4 21.9 %all_gather.11 = bf16[512,128]{1,0:T(8,128)(2,1)S(1)} all-gather(bf16[64,128]{1,0:T(8,128)(2,1)S(1)} %convolution_convert_fusion), channel_id=1, replica_groups=mesh['blk'=64,'rep'=8] {'rep'}, dimensions={0}, use_global_device_ids=true | all-gather | bytes 147456 | tf_op jit(solution)/shard_map/all_gather | solution.py:73
  160.3 4.8 convolution_bitcast_fusion
  165.2 112.6 %reduce-scatter.6.cloned.1.call-done = f32[1,512,128]{2,1,0:T(8,128)} async-done(((f32[8,512,128]{2,1,0:T(8,128)}), f32[1,512,128]{2,1,0:T(8,128)}) %reduce-scatter.6.cloned.1.call-update) | async-done | bytes 262160 | tf_op jit(solution)/shard_map/reduce_scatter | solution.py:77
  277.8 1.6 collective-permute-start.1
  279.4 0.9 fusion.22
  280.3 0.7 copy-done.2
  281.1 80.8 %all-reduce.3.cloned.1.call-done = f32[128,256]{1,0:T(8,128)} async-done(((f32[128,256]{1,0:T(8,128)}), f32[128,256]{1,0:T(8,128)}) %all-reduce.3.cloned.1.call-update) | async-done | bytes 131088 | tf_op jit(solution)/shard_map/psum | solution.py:69
  361.9 45.1 %reduce-scatter.8.cloned.1.call-done = f32[64,128]{1,0:T(8,128)} async-done(((f32[512,128]{1,0:T(8,128)}), f32[64,128]{1,0:T(8,128)}) %reduce-scatter.8.cloned.1.call-update) | async-done | bytes 32784 | tf_op jit(solution)/shard_map/reduce_scatter | solution.py:79
  407.0 1.4 convert_element_type.32
  408.4 498.8 %all-reduce.5.cloned.1.call-done = f32[128,256]{1,0:T(8,128)} async-done(((f32[128,256]{1,0:T(8,128)}), f32[128,256]{1,0:T(8,128)}) %all-reduce.5.cloned.1.call-update) | async-done | bytes 131088 | tf_op jit(solution)/shard_map/psum | solution.py:69
  907.1 1.6 copy.22
  (28 shorter events, 0.5 us)
Async XLA Ops:
  7.2 6.3 copy-start
  7.2 87.7 %all-gather.3.cloned.1.call-start = ((), (), s32[]{:S(2)}) async-start(), calls=%async_computation.8 | async-start | bytes 1179648 | tf_op jit(solution)/shard_map/all_gather | solution.py:53
  7.2 1.8 collective-permute-start
  9.0 0.7 copy-start.3
  9.7 126.0 %reduce-scatter.4.cloned.1.call-start = ((), (), s32[]{:S(2)}) async-start(), calls=%async_computation.3 | async-start | bytes 294912 | tf_op jit(solution)/shard_map/reduce_scatter | solution.py:58
  99.4 178.4 %reduce-scatter.6.cloned.1.call-start = ((), (), s32[]{:S(2)}) async-start(), calls=%async_computation.4 | async-start | bytes 2359296 | tf_op jit(solution)/shard_map/reduce_scatter | solution.py:77
  99.4 36.3 %copy-start.1 = (bf16[128,256]{1,0:T(8,128)(2,1)S(1)}, bf16[128,256]{1,0:T(8,128)(2,1)}, u32[]{:S(2)}) copy-start(bf16[128,256]{1,0:T(8,128)(2,1)} %param.7) | copy-start | bytes 196612
  99.4 37.2 %copy-start.5 = (bf16[64,256]{1,0:T(8,128)(2,1)S(1)}, bf16[64,256]{1,0:T(8,128)(2,1)}, u32[]{:S(2)}) copy-start(bf16[64,256]{1,0:T(8,128)(2,1)} %param.11) | copy-start | bytes 98308
  160.3 119.0 %copy-start.4 = (f32[64,128]{1,0:T(8,128)S(1)}, f32[64,128]{1,0:T(8,128)}, u32[]{:S(2)}) copy-start(f32[64,128]{1,0:T(8,128)} %reduce-scatter.4.cloned.1.call-done) | copy-start | bytes 98308
  165.2 196.7 %all-reduce.3.cloned.1.call-start = ((), (), s32[]{:S(2)}) async-start(), calls=%async_computation.6 | async-start | bytes 262144 | tf_op jit(solution)/shard_map/psum | solution.py:69
  277.8 2.5 collective-permute-start.1
  280.2 126.8 %reduce-scatter.8.cloned.1.call-start = ((), (), s32[]{:S(2)}) async-start(), calls=%async_computation.5 | async-start | bytes 294912 | tf_op jit(solution)/shard_map/reduce_scatter | solution.py:79
  280.3 0.7 copy-start.2
  281.0 626.1 %all-reduce.5.cloned.1.call-start = ((), (), s32[]{:S(2)}) async-start(), calls=%async_computation.7 | async-start | bytes 262144 | tf_op jit(solution)/shard_map/psum | solution.py:69
Sparse Core Ops, SparseCore 0:
  11.8 83.0 all-gather.2
  99.5 36.1 reduce-scatter.3
  165.3 112.4 reduce-scatter.5
  281.1 80.7 all-reduce.2
  364.5 42.4 reduce-scatter.7
  409.8 497.3 all-reduce.4
where the time goes:
time: 916 us
  waiting for transfers between devices  839 us (92%)
  blocking collectives  21.9 us (2%)
  local copies, waits for them, and re-layouts  17 us (2%)
  between operations  14.2 us (2%)
  matrix products  12.8 us (1%)
    psum x2, waiting for transfers between devices, local(): weight_grad = lax.psum(lax.psum(weight_grad, 'rep'), 'blk')  580 us
    reduce_scatter x1, waiting for transfers between devices, local(): lax.psum_scatter(partial, 'blk', scatter_dimension=0, axis_index_groups=r...  113 us
    all_gather x1, waiting for transfers between devices, local(): lax.all_gather(skewed(features, 1), 'blk', axis_index_groups=rings)  72.2 us
    reduce_scatter x1, waiting for transfers between devices, local(): lax.psum_scatter(partial, 'rep', scatter_dimension=0, tiled=True)  45.1 us
    reduce_scatter x1, waiting for transfers between devices, local(): mixed = lax.psum_scatter(mixed, 'rep', scatter_dimension=0, tiled=True)  29.8 us
    all_gather x1, blocking collectives, local(): lax.all_gather(row_grad, 'rep', axis=0, tiled=True)  21.9 us
  transfers between devices with their start and end apart: 8, of which 6 were waited for; matrix products, arithmetic and copies ran while one was open for 2% of the time, Pallas kernels for 0%

commit v1 on v0

--- a/solution.py
+++ b/solution.py
@@ -70,7 +70,9 @@
     row_grad = lax.dot_general(
         pre_grad, weight, (((1,), (1,)), ((), ())), preferred_element_type=jnp.float32
     ).astype(jnp.bfloat16)
-    row_grad = lax.all_gather(row_grad, "rep", axis=0, tiled=True).reshape(blocks, tile_size, feat)
+    row_grad = jnp.concatenate(
+        lax.all_to_all(jnp.stack([row_grad] * lax.axis_size("rep")), "rep", 0, 0), axis=0
+    ).reshape(blocks, tile_size, feat)
     partial = jnp.einsum(
         "jnmik,nif->jmkf", adjacency, row_grad, preferred_element_type=jnp.float32
     ).reshape(-1, rows, feat)

time: 916 us -> 900 us (0.983)
  blocking collectives: 21.9 us -> 0 us
    all_gather x1 -> x0, blocking collectives: 21.9 us -> none  [local(): lax.all_gather(row_grad, 'rep', axis=0, tiled=True)]
  transfers between devices with their start and end apart: 8 -> 9, of which waited for: 6 -> 6; matrix products, arithmetic and copies ran while one was open for 2% -> 2% of each run, Pallas kernels for 0% -> 0%
where the time goes in v1:
time: 900 us
  waiting for transfers between devices  841 us (93%)
  local copies, waits for them, and re-layouts  17.7 us (2%)
  between operations  14.2 us (2%)
  matrix products  12.7 us (1%)
    psum x2, waiting for transfers between devices, local(): weight_grad = lax.psum(lax.psum(weight_grad, 'rep'), 'blk')  579 us
    reduce_scatter x1, waiting for transfers between devices, local(): lax.psum_scatter(partial, 'blk', scatter_dimension=0, axis_index_groups=r...  108 us
    all_gather x1, waiting for transfers between devices, local(): lax.all_gather(skewed(features, 1), 'blk', axis_index_groups=rings)  72.2 us
    reduce_scatter x1, waiting for transfers between devices, local(): lax.psum_scatter(partial, 'rep', scatter_dimension=0, tiled=True)  45.1 us
    reduce_scatter x1, waiting for transfers between devices, local(): mixed = lax.psum_scatter(mixed, 'rep', scatter_dimension=0, tiled=True)  36.4 us
  transfers between devices with their start and end apart: 9, of which 6 were waited for; matrix products, arithmetic and copies ran while one was open for 2% of the time, Pallas kernels for 0%

profile of v1, /device:TPU:1, one launch (start us, length us, event | category | flops | bytes accessed | tf_op | source)
XLA Modules:
  0.0 899.5 jit_solution(6040555237820607740)
XLA Ops:
  7.2 1.8 collective-permute-start
  9.0 0.7 copy-done.3
  9.8 0.8 copy.13
  10.6 0.7 iota_compare_fusion.1
  11.2 0.7 iota_reduce_fusion
  11.9 0.6 gather_fusion.1
  12.6 0.1 fusion.13
  12.7 0.6 gather_fusion
  13.3 0.1 copy.14
  13.4 0.1 copy.15
  13.5 3.1 gather_fusion.2
  16.6 3.9 fusion
  20.5 2.3 copy.16
  22.7 72.2 %all-gather.3.cloned.1.call-done = bf16[4096,128]{1,0:T(8,128)(2,1)} async-done(((bf16[512,128]{1,0:T(8,128)(2,1)}), bf16[4096,128]{1,0:T(8,128)(2,1)}) %all-gather.3.cloned.1.call-update) | async-done | bytes 1048592 | tf_op jit(solution)/shard_map/all_gather | solution.py:53
  94.9 4.4 convolution_bitcast_fusion.1
  99.4 36.4 %reduce-scatter.4.cloned.1.call-done = f32[64,128]{1,0:T(8,128)} async-done(((f32[512,128]{1,0:T(8,128)}), f32[64,128]{1,0:T(8,128)}) %reduce-scatter.4.cloned.1.call-update) | async-done | bytes 32784 | tf_op jit(solution)/shard_map/reduce_scatter | solution.py:58
  135.7 0.9 fusion.25
  136.6 1.6 fusion.4
  138.3 0.1 convolution_convert_fusion
  138.4 0.7 stack.2
  139.1 3.4 all-to-all-start
  142.5 6.5 copy.17
  149.0 4.8 convolution_bitcast_fusion
  153.9 108.0 %reduce-scatter.6.cloned.1.call-done = f32[1,512,128]{2,1,0:T(8,128)} async-done(((f32[8,512,128]{2,1,0:T(8,128)}), f32[1,512,128]{2,1,0:T(8,128)}) %reduce-scatter.6.cloned.1.call-update) | async-done | bytes 262160 | tf_op jit(solution)/shard_map/reduce_scatter | solution.py:79
  261.9 1.6 collective-permute-start.1
  263.5 0.9 fusion.22
  264.4 0.7 copy-done.2
  265.2 80.7 %all-reduce.3.cloned.1.call-done = f32[128,256]{1,0:T(8,128)} async-done(((f32[128,256]{1,0:T(8,128)}), f32[128,256]{1,0:T(8,128)}) %all-reduce.3.cloned.1.call-update) | async-done | bytes 131088 | tf_op jit(solution)/shard_map/psum | solution.py:69
  345.9 45.1 %reduce-scatter.8.cloned.1.call-done = f32[64,128]{1,0:T(8,128)} async-done(((f32[512,128]{1,0:T(8,128)}), f32[64,128]{1,0:T(8,128)}) %reduce-scatter.8.cloned.1.call-update) | async-done | bytes 32784 | tf_op jit(solution)/shard_map/reduce_scatter | solution.py:81
  391.0 1.4 convert_element_type.32
  392.4 498.8 %all-reduce.5.cloned.1.call-done = f32[128,256]{1,0:T(8,128)} async-done(((f32[128,256]{1,0:T(8,128)}), f32[128,256]{1,0:T(8,128)}) %all-reduce.5.cloned.1.call-update) | async-done | bytes 131088 | tf_op jit(solution)/shard_map/psum | solution.py:69
  891.1 1.6 copy.22
  (30 shorter events, 0.6 us)
Async XLA Ops:
  7.2 6.3 copy-start
  7.2 87.7 %all-gather.3.cloned.1.call-start = ((), (), s32[]{:S(2)}) async-start(), calls=%async_computation.9 | async-start | bytes 1179648 | tf_op jit(solution)/shard_map/all_gather | solution.py:53
  7.2 1.8 collective-permute-start
  9.0 0.7 copy-start.3
  9.7 126.0 %reduce-scatter.4.cloned.1.call-start = ((), (), s32[]{:S(2)}) async-start(), calls=%async_computation.4 | async-start | bytes 294912 | tf_op jit(solution)/shard_map/reduce_scatter | solution.py:58
  22.7 113.0 %copy-start.1 = (bf16[128,256]{1,0:T(8,128)(2,1)S(1)}, bf16[128,256]{1,0:T(8,128)(2,1)}, u32[]{:S(2)}) copy-start(bf16[128,256]{1,0:T(8,128)(2,1)} %param.7) | copy-start | bytes 196612
  22.7 113.9 %copy-start.5 = (bf16[64,256]{1,0:T(8,128)(2,1)S(1)}, bf16[64,256]{1,0:T(8,128)(2,1)}, u32[]{:S(2)}) copy-start(bf16[64,256]{1,0:T(8,128)(2,1)} %param.11) | copy-start | bytes 98308
  139.1 9.9 %all-to-all-start = ((bf16[8,64,128]{2,1,0:T(8,128)(2,1)}), bf16[8,64,128]{2,1,0:T(8,128)(2,1)S(1)}, u32[]{:S(2)}, u32[]{:S(2)}) async-start(bf16[8,64,128]{2,1,0:T(8,128)(2,1)} %stack.2), calls=%async_computation.1 | async-start | bytes 262144 | tf_op jit(solution)/shard_map/all_to_all | solution.py:74
  142.5 119.4 %reduce-scatter.6.cloned.1.call-start = ((), (), s32[]{:S(2)}) async-start(), calls=%async_computation.5 | async-start | bytes 2359296 | tf_op jit(solution)/shard_map/reduce_scatter | solution.py:79
  149.0 114.4 %copy-start.4 = (f32[64,128]{1,0:T(8,128)S(1)}, f32[64,128]{1,0:T(8,128)}, u32[]{:S(2)}) copy-start(f32[64,128]{1,0:T(8,128)} %reduce-scatter.4.cloned.1.call-done) | copy-start | bytes 98308
  153.9 192.0 %all-reduce.3.cloned.1.call-start = ((), (), s32[]{:S(2)}) async-start(), calls=%async_computation.7 | async-start | bytes 262144 | tf_op jit(solution)/shard_map/psum | solution.py:69
  261.9 2.5 collective-permute-start.1
  264.4 126.6 %reduce-scatter.8.cloned.1.call-start = ((), (), s32[]{:S(2)}) async-start(), calls=%async_computation.6 | async-start | bytes 294912 | tf_op jit(solution)/shard_map/reduce_scatter | solution.py:81
  264.4 0.7 copy-start.2
  265.1 626.0 %all-reduce.5.cloned.1.call-start = ((), (), s32[]{:S(2)}) async-start(), calls=%async_computation.8 | async-start | bytes 262144 | tf_op jit(solution)/shard_map/psum | solution.py:69
Sparse Core Ops, SparseCore 0:
  11.8 83.0 all-gather.2
  99.5 36.1 reduce-scatter.3
  154.0 107.8 reduce-scatter.5
  265.2 80.6 all-reduce.2
  348.5 42.4 reduce-scatter.7
  393.8 497.3 all-reduce.4

commit v2 on v0

--- a/solution.py
+++ b/solution.py
@@ -66,7 +66,7 @@
         (((0,), (0,)), ((), ())),
         preferred_element_type=jnp.float32,
     )
-    weight_grad = lax.psum(lax.psum(weight_grad, "rep"), "blk")
+    weight_grad = lax.psum(jnp.sum(lax.all_gather(weight_grad, "rep"), axis=0), "blk")
     row_grad = lax.dot_general(
         pre_grad, weight, (((1,), (1,)), ((), ())), preferred_element_type=jnp.float32
     ).astype(jnp.bfloat16)

time: 916 us -> 872 us (0.952)
  waiting for transfers between devices: 839 us -> 793 us
    psum x2 -> x1, waiting for transfers between devices: 580 us -> 499 us  [local(): lax.psum(jnp.sum(lax.all_gather(weight_grad, 'rep'), axis=0), 'blk')]
    all_gather x0 -> x1, waiting for transfers between devices: none -> 37.6 us  [local(): lax.all_gather(weight_grad, 'rep')]
  transfers between devices with their start and end apart: 8 -> 8, of which waited for: 6 -> 6; matrix products, arithmetic and copies ran while one was open for 2% -> 3% of each run, Pallas kernels for 0% -> 0%
where the time goes in v2:
time: 872 us
  waiting for transfers between devices  793 us (91%)
  blocking collectives  21.9 us (3%)
  local copies, waits for them, and re-layouts  17 us (2%)
  between operations  14.2 us (2%)
  matrix products  12.8 us (1%)
    psum x1, waiting for transfers between devices, local(): lax.psum(jnp.sum(lax.all_gather(weight_grad, 'rep'), axis=0), 'blk')  499 us
    reduce_scatter x1, waiting for transfers between devices, local(): lax.psum_scatter(partial, 'blk', scatter_dimension=0, axis_index_groups=r...  111 us
    all_gather x1, waiting for transfers between devices, local(): lax.all_gather(skewed(features, 1), 'blk', axis_index_groups=rings)  72.2 us
    reduce_scatter x1, waiting for transfers between devices, local(): lax.psum_scatter(partial, 'rep', scatter_dimension=0, tiled=True)  43 us
    all_gather x1, waiting for transfers between devices, local(): lax.all_gather(weight_grad, 'rep')  37.6 us
    reduce_scatter x1, waiting for transfers between devices, local(): mixed = lax.psum_scatter(mixed, 'rep', scatter_dimension=0, tiled=True)  29.8 us
    all_gather x1, blocking collectives, local(): lax.all_gather(row_grad, 'rep', axis=0, tiled=True)  21.9 us
  transfers between devices with their start and end apart: 8, of which 6 were waited for; matrix products, arithmetic and copies ran while one was open for 3% of the time, Pallas kernels for 0%

profile of v2, /device:TPU:1, one launch (start us, length us, event | category | flops | bytes accessed | tf_op | source)
XLA Modules:
  0.0 871.6 jit_solution(17729844135521476849)
XLA Ops:
  7.2 1.8 collective-permute-start
  9.0 0.7 copy-done.3
  9.8 0.8 copy.13
  10.6 0.7 iota_compare_fusion.1
  11.2 0.7 iota_reduce_fusion
  11.9 0.6 gather_fusion.1
  12.6 0.1 fusion.13
  12.7 0.6 gather_fusion
  13.3 0.1 copy.14
  13.4 0.1 copy.15
  13.5 3.1 gather_fusion.2
  16.6 3.9 fusion
  20.5 2.3 copy.16
  22.7 72.2 %all-gather.5.cloned.1.call-done = bf16[4096,128]{1,0:T(8,128)(2,1)} async-done(((bf16[512,128]{1,0:T(8,128)(2,1)}), bf16[4096,128]{1,0:T(8,128)(2,1)}) %all-gather.5.cloned.1.call-update) | async-done | bytes 1048592 | tf_op jit(solution)/shard_map/all_gather | solution.py:53
  94.9 4.4 convolution_bitcast_fusion.1
  99.5 6.5 copy.17
  105.9 29.8 %reduce-scatter.4.cloned.1.call-done = f32[64,128]{1,0:T(8,128)} async-done(((f32[512,128]{1,0:T(8,128)}), f32[64,128]{1,0:T(8,128)}) %reduce-scatter.4.cloned.1.call-update) | async-done | bytes 32784 | tf_op jit(solution)/shard_map/reduce_scatter | solution.py:58
  135.7 0.9 fusion.25
  136.6 1.6 fusion.4
  138.3 0.1 convolution_convert_fusion
  138.4 21.9 %all_gather.17 = bf16[512,128]{1,0:T(8,128)(2,1)S(1)} all-gather(bf16[64,128]{1,0:T(8,128)(2,1)S(1)} %convolution_convert_fusion), channel_id=1, replica_groups=mesh['blk'=64,'rep'=8] {'rep'}, dimensions={0}, use_global_device_ids=true | all-gather | bytes 147456 | tf_op jit(solution)/shard_map/all_gather | solution.py:73
  160.3 4.8 convolution_bitcast_fusion
  165.2 0.9 fusion.22
  166.2 111.4 %reduce-scatter.6.cloned.1.call-done = f32[1,512,128]{2,1,0:T(8,128)} async-done(((f32[8,512,128]{2,1,0:T(8,128)}), f32[1,512,128]{2,1,0:T(8,128)}) %reduce-scatter.6.cloned.1.call-update) | async-done | bytes 262160 | tf_op jit(solution)/shard_map/reduce_scatter | solution.py:77
  277.5 1.6 collective-permute-start.1
  279.1 0.7 copy-done.2
  279.9 37.6 %all-gather.7.cloned.1.call-done = f32[1024,256]{1,0:T(8,128)} async-done(((f32[128,256]{1,0:T(8,128)}), f32[1024,256]{1,0:T(8,128)}) %all-gather.7.cloned.1.call-update) | async-done | bytes 1048592 | tf_op jit(solution)/shard_map/all_gather | solution.py:69
  317.5 2.0 reduce_sum.9
  319.5 43.0 %reduce-scatter.8.cloned.1.call-done = f32[64,128]{1,0:T(8,128)} async-done(((f32[512,128]{1,0:T(8,128)}), f32[64,128]{1,0:T(8,128)}) %reduce-scatter.8.cloned.1.call-update) | async-done | bytes 32784 | tf_op jit(solution)/shard_map/reduce_scatter | solution.py:79
  362.4 1.4 convert_element_type.32
  363.8 499.4 %all-reduce.2.cloned.1.call-done = f32[128,256]{1,0:T(8,128)} async-done(((f32[128,256]{1,0:T(8,128)}), f32[128,256]{1,0:T(8,128)}) %all-reduce.2.cloned.1.call-update) | async-done | bytes 131088 | tf_op jit(solution)/shard_map/psum | solution.py:69
  863.2 1.6 copy.21
  (29 shorter events, 0.6 us)
Async XLA Ops:
  7.2 6.3 copy-start
  7.2 87.7 %all-gather.5.cloned.1.call-start = ((), (), s32[]{:S(2)}) async-start(), calls=%async_computation.7 | async-start | bytes 1179648 | tf_op jit(solution)/shard_map/all_gather | solution.py:53
  7.2 1.8 collective-permute-start
  9.0 0.7 copy-start.3
  9.7 126.0 %reduce-scatter.4.cloned.1.call-start = ((), (), s32[]{:S(2)}) async-start(), calls=%async_computation.3 | async-start | bytes 294912 | tf_op jit(solution)/shard_map/reduce_scatter | solution.py:58
  99.4 178.1 %reduce-scatter.6.cloned.1.call-start = ((), (), s32[]{:S(2)}) async-start(), calls=%async_computation.4 | async-start | bytes 2359296 | tf_op jit(solution)/shard_map/reduce_scatter | solution.py:77
  99.4 36.3 %copy-start.1 = (bf16[128,256]{1,0:T(8,128)(2,1)S(1)}, bf16[128,256]{1,0:T(8,128)(2,1)}, u32[]{:S(2)}) copy-start(bf16[128,256]{1,0:T(8,128)(2,1)} %param.7) | copy-start | bytes 196612
  99.4 37.2 %copy-start.5 = (bf16[64,256]{1,0:T(8,128)(2,1)S(1)}, bf16[64,256]{1,0:T(8,128)(2,1)}, u32[]{:S(2)}) copy-start(bf16[64,256]{1,0:T(8,128)(2,1)} %param.11) | copy-start | bytes 98308
  160.3 4.9 copy-start.4
  165.2 152.3 %all-gather.7.cloned.1.call-start = ((), (), s32[]{:S(2)}) async-start(), calls=%async_computation.8 | async-start | bytes 1179648 | tf_op jit(solution)/shard_map/all_gather | solution.py:69
  166.1 196.3 %reduce-scatter.8.cloned.1.call-start = ((), (), s32[]{:S(2)}) async-start(), calls=%async_computation.5 | async-start | bytes 294912 | tf_op jit(solution)/shard_map/reduce_scatter | solution.py:79
  277.5 1.6 collective-permute-start.1
  279.1 0.7 copy-start.2
  279.8 583.4 %all-reduce.2.cloned.1.call-start = ((), (), s32[]{:S(2)}) async-start(), calls=%async_computation.6 | async-start | bytes 262144 | tf_op jit(solution)/shard_map/psum | solution.py:69
Sparse Core Ops, SparseCore 0:
  11.8 83.0 all-gather.4
  99.5 36.1 reduce-scatter.3
  165.3 112.1 reduce-scatter.5
  280.0 37.4 all-gather.6
  320.1 42.2 reduce-scatter.7
  365.8 497.3 all-reduce.1
